TPU v7x, 256 devices: a whole 4x4x8 slice. The times are simulated.
256 devices in a mesh: grp: 8 (over z_hi, core), dev: 32 (over z_lo, y, x).
Axes of the slice: x: 4, y: 4, z: 8 (z_hi: 4, z_lo: 2; z = z_hi * 2 + z_lo), core: 2. Of those that a mesh axis runs over, the one named last changes fastest.
Arguments:
- user_factors: float32 [32768, 256], P(('grp', 'dev')), may hold values from -0.5 to 0.5
- item_factors: float32 [16384, 256], P(('grp', 'dev')), may hold values from -0.5 to 0.5
- user_items: int32 [32768, 8, 3], P(('grp', 'dev')), may hold values from 0 to 2047, as said below
- user_conf: float32 [32768, 8, 3], P(('grp', 'dev')), may hold values from 1 to 200
- user_mask: int32 [32768, 8, 3], P(('grp', 'dev')), may hold values 0 or 1
- item_users: int32 [16384, 8, 6], P(('grp', 'dev')), may hold values from 0 to 4095, as said below
- item_conf: float32 [16384, 8, 6], P(('grp', 'dev')), may hold values from 1 to 200
- item_mask: int32 [16384, 8, 6], P(('grp', 'dev')), may hold values 0 or 1
Outputs:
- new_users: float32 [32768, 256], P(('grp', 'dev'))
- new_items: float32 [16384, 256], P(('grp', 'dev'))
Inputs may be any that keep to these rules, and one draw needn't show every extreme that they name: Within owner block c, id // 64 is the owner device and id % 64 its row. The user_items of the users of one device, in one owner block, name at most 16 distinct rows of any one owner device, and in every block each device names exactly 16 distinct rows of some owner device. Within owner block c, id // 128 is the owner device and id % 128 its row. The item_users of the items of one device, in one owner block, name at most 16 distinct rows of any one owner device, and in every block each device names exactly 16 distinct rows of some owner device.
All inputs are finite; a program needn't handle non-finite values. No bound on the sum of `user_mask` or of `item_mask` on one device may be relied on, other than what follows from the above.
Results may differ from a plain program's by a relative error of at most 0.0044.
Values may be sent and summed in bfloat16 or wider, within the bound.
A program may use at most 128 MiB of HBM per device.

v0:
```python
import jax
import jax.numpy as jnp
from jax import lax
from jax.sharding import Mesh
from jax.sharding import PartitionSpec as P

CG_STEPS = 4
GRP = ("grp_0", "grp_1")
GRP_DEV = ("grp_0", "grp_1", "dev")
ridge = 1.0


def joined_along(blocks, dim):
    dims = list(blocks.shape[1:])
    dims[dim] *= blocks.shape[0]
    return jnp.moveaxis(blocks, 0, dim).reshape(dims)


def gather_in_order(array, axes, turns):
    blocks = array
    for k in turns:
        blocks = lax.all_gather(blocks, axes[k])
    done = turns[::-1]
    back = [done.index(k) for k in range(len(axes))]
    blocks = blocks.transpose(*back, *range(len(axes), blocks.ndim))
    return blocks.reshape(-1, *array.shape)


def whole_of(array, axes, turns, dim):
    return joined_along(gather_in_order(array, axes, turns), dim)


def solve_rows(gram, start_x, rows, confidence, slot_mask):
    maskf = slot_mask.astype(jnp.float32)
    weight = confidence * maskf
    rhs = jnp.einsum(
        "us,usr->ur", maskf * (1.0 + confidence), rows, precision=lax.Precision.HIGHEST
    )

    def apply(vector):
        along = jnp.einsum("usr,ur->us", rows, vector, precision=lax.Precision.HIGHEST)
        extra = jnp.einsum("us,usr->ur", weight * along, rows, precision=lax.Precision.HIGHEST)
        return jnp.dot(vector, gram, precision=lax.Precision.HIGHEST) + ridge * vector + extra

    solution = start_x
    resid = rhs - apply(solution)
    direction = resid
    norm_now = jnp.sum(resid * resid, axis=1, keepdims=True)
    for step in range(CG_STEPS):
        image = apply(direction)
        alpha = norm_now / jnp.sum(direction * image, axis=1, keepdims=True)
        solution = solution + alpha * direction
        resid = resid - alpha * image
        norm_next = jnp.sum(resid * resid, axis=1, keepdims=True)
        direction = resid + norm_next / norm_now * direction
        norm_now = norm_next
    return solution


def gram_of(block):
    return lax.dot_general(
        block, block, (((0,), (0,)), ((), ())), preferred_element_type=jnp.float32
    )


def collect(whole, row_index, mask_now):
    picked = jnp.take(whole, row_index, axis=0).astype(jnp.float32)
    return picked * mask_now[..., None].astype(jnp.float32)


def half_step(start_x, other, slot_ids, confidence, slot_mask):
    local_rows = other.shape[0]
    groups = lax.axis_size(GRP)
    packed = other.astype(jnp.bfloat16)
    row_parts = []
    conf_parts = []
    mask_parts = []
    stacked = whole_of(packed, GRP, (0, 1), 0)
    whole = lax.all_gather(stacked, "dev", axis=0, tiled=True)
    for span in range(groups):
        local = slot_ids[:, span, :]
        row_index = (
            local // local_rows * (groups * local_rows) + span * local_rows + local % local_rows
        )
        row_parts.append(collect(whole, row_index, slot_mask[:, span, :]))
        conf_parts.append(confidence[:, span, :])
        mask_parts.append(slot_mask[:, span, :])
    squares = gram_of(whole)
    rows = jnp.concatenate(row_parts, axis=1)
    conf_all = jnp.concatenate(conf_parts, axis=1)
    mask_all = jnp.concatenate(mask_parts, axis=1)
    return solve_rows(squares, start_x, rows, conf_all, mask_all)


def per_device(
    user_factors, item_factors, user_items, user_conf, user_mask, item_users, item_conf, item_mask
):
    new_users = half_step(user_factors, item_factors, user_items, user_conf, user_mask)
    new_items = half_step(item_factors, new_users, item_users, item_conf, item_mask)
    return (new_users, new_items)


def solution(mesh):
    finer = Mesh(mesh.devices.reshape(4, 2, mesh.shape["dev"]), ("grp_0", "grp_1", "dev"))
    in_specs = (
        P(GRP_DEV, None),
        P(GRP_DEV, None),
        P(GRP_DEV, None, None),
        P(GRP_DEV, None, None),
        P(GRP_DEV, None, None),
        P(GRP_DEV, None, None),
        P(GRP_DEV, None, None),
        P(GRP_DEV, None, None),
    )
    out_specs = (P(GRP_DEV, None), P(GRP_DEV, None))
    return jax.shard_map(
        per_device, mesh=finer, in_specs=in_specs, out_specs=out_specs, check_vma=False
    )
```

profile of v0, /device:TPU:1, one launch (start us, length us, event | category | flops | bytes accessed | tf_op | source)
XLA Modules:
  0.0 744.5 jit_solution(14757438769674752799)
XLA Ops:
  8.1 15.5 %all-gather = bf16[256,256]{1,0:T(8,128)(2,1)S(1)} all-gather(bf16[64,256]{1,0:T(8,128)(2,1)S(1)} %convert_element_type.189), channel_id=2, replica_groups=mesh['grp_0'=4,'grp_1'=2,'dev'=32] {'grp_0'}, dimensions={0}, use_global_device_ids=true | all-gather | bytes 163840 | tf_op jit(solution)/shard_map/all_gather | solution.py:22
  23.6 5.0 all-gather.1
  38.0 139.0 %all-gather.7.cloned.1.call-done = bf16[16384,256]{1,0:T(8,128)(2,1)} async-done(((bf16[512,256]{1,0:T(8,128)(2,1)}), bf16[16384,256]{1,0:T(8,128)(2,1)}) %all-gather.7.cloned.1.call-update) | async-done | bytes 8388624 | tf_op jit(solution)/shard_map/all_gather | solution.py:79
  177.0 6.1 gather_fusion.7
  183.2 6.1 gather_fusion.6
  189.5 6.1 gather_fusion.5
  195.7 6.1 gather_fusion.4
  202.0 6.1 gather_fusion.3
  208.2 6.7 gather_fusion.2
  215.0 6.1 gather_fusion.1
  221.2 6.1 gather_fusion
  236.6 22.3 %concatenate.20 = f32[128,24,256]{2,1,0:T(8,128)S(1)} concatenate(f32[128,3,256]{2,1,0:T(4,128)} %convert_multiply_fusion.15, f32[128,3,256]{2,1,0:T(4,128)} %convert_multiply_fusion.14, f32[128,3,256]{2,1,0:T(4,128)} %convert_multiply_fusion.13, f32[128,3,256]{2,1,0:T(4,128)} %convert_multiply_fusion.12, f32[128,3,256]{2,1,0:T(4,128)} %convert_multiply_fusion.11, ...), dimensions={1} | concatenate | bytes 6291456 | tf_op jit(solution)/shard_map/concatenate | solution.py:89
  258.9 2.8 fusion.18
  264.8 8.2 %fusion.190 = f32[256,256]{1,0:T(8,128)S(1)} fusion(bf16[16384,256]{1,0:T(8,128)(2,1)} %all-gather.7.cloned.1.call-done), kind=kOutput, calls=%fused_computation.457 | convolution fusion | flops 2147483648 | bytes 8650752 | tf_op jit(solution)/shard_map/dot_general | solution.py:61
  337.5 13.1 %all-gather.2 = bf16[512,256]{0,1:T(8,128)(2,1)S(1)} all-gather(bf16[128,256]{0,1:T(8,128)(2,1)S(1)} %get-tuple-element.36), channel_id=4, replica_groups=mesh['grp_0'=4,'grp_1'=2,'dev'=32] {'grp_0'}, dimensions={0}, use_global_device_ids=true | all-gather | bytes 327680 | tf_op jit(solution)/shard_map/all_gather | solution.py:22
  350.7 25.6 %all-gather.3 = bf16[8,128,256]{2,1,0:T(8,128)(2,1)S(1)} all-gather(bf16[4,128,256]{2,1,0:T(8,128)(2,1)S(1)} %bitcast.642), channel_id=5, replica_groups=mesh['grp_0'=4,'grp_1'=2,'dev'=32] {'grp_1'}, dimensions={0}, use_global_device_ids=true | all-gather | bytes 786432 | tf_op jit(solution)/shard_map/all_gather | solution.py:22
  383.0 185.0 %all-gather.9.cloned.1.call-done = bf16[32768,256]{1,0:T(8,128)(2,1)} async-done(((bf16[1024,256]{1,0:T(8,128)(2,1)}), bf16[32768,256]{1,0:T(8,128)(2,1)}) %all-gather.9.cloned.1.call-update) | async-done | bytes 16777232 | tf_op jit(solution)/shard_map/all_gather | solution.py:79
  568.0 9.6 %gather_fusion.15 = bf16[384,256]{1,0:T(8,128)(2,1)S(1)} fusion(bf16[32768,256]{1,0:T(8,128)(2,1)} %all-gather.9.cloned.1.call-done, s32[1024]{0:T(1024)S(1)} %pad_clamp_fusion), kind=kCustom, calls=%fused_computation.15.clone | custom fusion | bytes 394752 | tf_op jit(solution)/shard_map/jit(_take)/gather | solution.py:67
  577.7 9.6 %gather_fusion.14 = bf16[384,256]{1,0:T(8,128)(2,1)S(1)} fusion(bf16[32768,256]{1,0:T(8,128)(2,1)} %all-gather.9.cloned.1.call-done, s32[1024]{0:T(1024)S(1)} %pad_clamp_fusion.1), kind=kCustom, calls=%fused_computation.14.clone | custom fusion | bytes 394752 | tf_op jit(solution)/shard_map/jit(_take)/gather | solution.py:67
  587.4 9.6 %gather_fusion.13 = bf16[384,256]{1,0:T(8,128)(2,1)S(1)} fusion(bf16[32768,256]{1,0:T(8,128)(2,1)} %all-gather.9.cloned.1.call-done, s32[1024]{0:T(1024)S(1)} %pad_clamp_fusion.2), kind=kCustom, calls=%fused_computation.13.clone | custom fusion | bytes 394752 | tf_op jit(solution)/shard_map/jit(_take)/gather | solution.py:67
  597.0 9.8 %gather_fusion.12 = bf16[384,256]{1,0:T(8,128)(2,1)S(1)} fusion(bf16[32768,256]{1,0:T(8,128)(2,1)} %all-gather.9.cloned.1.call-done, s32[1024]{0:T(1024)S(1)} %pad_clamp_fusion.3), kind=kCustom, calls=%fused_computation.12.clone | custom fusion | bytes 394752 | tf_op jit(solution)/shard_map/jit(_take)/gather | solution.py:67
  606.9 9.6 %gather_fusion.11 = bf16[384,256]{1,0:T(8,128)(2,1)S(1)} fusion(bf16[32768,256]{1,0:T(8,128)(2,1)} %all-gather.9.cloned.1.call-done, s32[1024]{0:T(1024)S(1)} %pad_clamp_fusion.4), kind=kCustom, calls=%fused_computation.11.clone | custom fusion | bytes 394752 | tf_op jit(solution)/shard_map/jit(_take)/gather | solution.py:67
  616.6 9.6 %gather_fusion.10 = bf16[384,256]{1,0:T(8,128)(2,1)S(1)} fusion(bf16[32768,256]{1,0:T(8,128)(2,1)} %all-gather.9.cloned.1.call-done, s32[1024]{0:T(1024)S(1)} %pad_clamp_fusion.5), kind=kCustom, calls=%fused_computation.10.clone | custom fusion | bytes 394752 | tf_op jit(solution)/shard_map/jit(_take)/gather | solution.py:67
  626.3 9.6 %gather_fusion.9 = bf16[384,256]{1,0:T(8,128)(2,1)S(1)} fusion(bf16[32768,256]{1,0:T(8,128)(2,1)} %all-gather.9.cloned.1.call-done, s32[1024]{0:T(1024)S(1)} %pad_clamp_fusion.6), kind=kCustom, calls=%fused_computation.9.clone | custom fusion | bytes 394752 | tf_op jit(solution)/shard_map/jit(_take)/gather | solution.py:67
  635.9 9.8 %gather_fusion.8 = bf16[384,256]{1,0:T(8,128)(2,1)S(1)} fusion(bf16[32768,256]{1,0:T(8,128)(2,1)} %all-gather.9.cloned.1.call-done, s32[1024]{0:T(1024)S(1)} %pad_clamp_fusion.7), kind=kCustom, calls=%fused_computation.1.clone | custom fusion | bytes 394752 | tf_op jit(solution)/shard_map/jit(_take)/gather | solution.py:67
  653.8 20.6 %concatenate.23 = f32[64,48,256]{2,1,0:T(8,128)S(1)} concatenate(f32[64,6,256]{2,1,0:T(8,128)} %convert_multiply_fusion.7, f32[64,6,256]{2,1,0:T(8,128)} %convert_multiply_fusion.6, f32[64,6,256]{2,1,0:T(8,128)} %convert_multiply_fusion.5, f32[64,6,256]{2,1,0:T(8,128)} %convert_multiply_fusion.4, f32[64,6,256]{2,1,0:T(8,128)} %convert_multiply_fusion.3, ...), dimensions={1} | concatenate | bytes 6291456 | tf_op jit(solution)/shard_map/concatenate | solution.py:89
  674.4 2.8 fusion.28
  682.0 14.5 %fusion.192 = f32[256,256]{1,0:T(8,128)S(1)} fusion(bf16[32768,256]{1,0:T(8,128)(2,1)} %all-gather.9.cloned.1.call-done), kind=kOutput, calls=%fused_computation.459 | convolution fusion | flops 4294967296 | bytes 17039360 | tf_op jit(solution)/shard_map/dot_general | solution.py:61
  696.8 2.8 fusion.26
  702.4 3.4 fusion.24
  714.3 3.4 fusion.22
  726.3 3.4 fusion.20
  (313 shorter events, 135.3 us)
Async XLA Ops:
  7.2 29.2 %copy-start.5 = (f32[128,256]{1,0:T(8,128)S(1)}, f32[128,256]{1,0:T(8,128)}, u32[]{:S(2)}) copy-start(f32[128,256]{1,0:T(8,128)} %param.12) | copy-start | bytes 393220
  7.2 29.9 %copy-start.23 = (f32[128,8,3]{0,1,2:T(8,128)S(1)}, f32[128,8,3]{0,1,2:T(8,128)}, u32[]{:S(2)}) copy-start(f32[128,8,3]{0,1,2:T(8,128)} %param.15) | copy-start | bytes 36868
  7.2 169.8 %all-gather.7.cloned.1.call-start = ((), (), s32[]{:S(2)}) async-start(), calls=%async_computation | async-start | bytes 8650752 | tf_op jit(solution)/shard_map/all_gather | solution.py:79
  29.4 538.6 %all-gather.9.cloned.1.call-start = ((), (), s32[]{:S(2)}) async-start(), calls=%async_computation.1 | async-start | bytes 17301504 | tf_op jit(solution)/shard_map/all_gather | solution.py:79
  264.8 8.2 %copy-start.6 = (f32[128,256]{1,0:T(8,128)S(1)}, f32[128,256]{1,0:T(8,128)}, u32[]{:S(2)}) copy-start(f32[128,256]{1,0:T(8,128)} %param.12) | copy-start | bytes 393220
  264.8 8.2 %copy-start.7 = (f32[128,256]{0,1:T(8,128)S(1)}, f32[128,256]{0,1:T(8,128)}, u32[]{:S(2)}) copy-start(f32[128,256]{0,1:T(8,128)} %copy.246) | copy-start | bytes 393220
  264.8 8.2 %copy-start.17 = (f32[128,256]{0,1:T(8,128)S(1)}, f32[128,256]{0,1:T(8,128)}, u32[]{:S(2)}) copy-start(f32[128,256]{0,1:T(8,128)} %copy.310) | copy-start | bytes 393220
  264.8 8.2 %copy-start.18 = (f32[128,256]{0,1:T(8,128)S(1)}, f32[128,256]{0,1:T(8,128)}, u32[]{:S(2)}) copy-start(f32[128,256]{0,1:T(8,128)} %copy.304) | copy-start | bytes 393220
  286.0 0.7 copy-start
  286.1 0.6 copy-start.26
  301.4 1.0 copy-start.25
  302.4 0.5 copy-start.27
  302.4 1.2 copy-start.1
  319.2 2.1 copy-start.24
  333.1 44.0 %copy-start.20 = (s32[64,8,6]{0,1,2:T(8,128)S(1)}, s32[64,8,6]{0,1,2:T(8,128)}, u32[]{:S(2)}) copy-start(s32[64,8,6]{0,1,2:T(8,128)} %param.17) | copy-start | bytes 36868
  333.1 45.1 %copy-start.21 = (s32[64,8,6]{0,1,2:T(8,128)S(1)}, s32[64,8,6]{0,1,2:T(8,128)}, u32[]{:S(2)}) copy-start(s32[64,8,6]{0,1,2:T(8,128)} %param.19) | copy-start | bytes 36868
  333.1 47.8 %copy-start.22 = (f32[64,8,6]{0,1,2:T(8,128)S(1)}, f32[64,8,6]{0,1,2:T(8,128)}, u32[]{:S(2)}) copy-start(f32[64,8,6]{0,1,2:T(8,128)} %param.18) | copy-start | bytes 36868
  653.8 20.6 %copy-start.14 = (f32[64,256]{1,0:T(8,128)S(1)}, f32[64,256]{1,0:T(8,128)}, u32[]{:S(2)}) copy-start(f32[64,256]{1,0:T(8,128)} %param.13) | copy-start | bytes 196612
  682.0 14.5 %copy-start.19 = (f32[64,1,256]{2,1,0:T(1,128)S(1)}, f32[64,1,256]{2,1,0:T(1,128)}, u32[]{:S(2)}) copy-start(f32[64,1,256]{2,1,0:T(1,128)} %fusion.193) | copy-start | bytes 196612
  696.8 2.8 copy-start.16
  701.7 0.6 copy-start.8
  710.0 2.8 copy-start.9
  713.0 0.6 copy-start.10
  713.7 0.6 copy-start.2
  722.0 2.6 copy-start.3
  722.0 3.0 copy-start.11
  725.1 0.6 copy-start.29
  725.7 0.6 copy-start.12
  726.3 10.4 %copy-start.30 = (f32[64]{0:T(128)S(1)}, f32[64]{0:T(128)}, u32[]{:S(2)}) copy-start(f32[64]{0:T(128)} %copy-done.29) | copy-start | bytes 772
  733.9 2.4 copy-start.13
  733.9 2.8 copy-start.4
  733.9 2.8 copy-start.15
  (1 other events, 0.5 us)
Sparse Core Ops, SparseCore 0:
  29.5 147.4 all-gather.6
  377.2 190.7 all-gather.8
where the time goes:
time: 751 us; the launch traced here: 745 us
  waiting for transfers between devices  324 us (43%)
  local copies, waits for them, and re-layouts  225 us (30%)
  matrix products  62.8 us (8%)
  blocking collectives  59.2 us (8%)
  other arithmetic  58.1 us (8%)
  between operations  15.2 us (2%)
    all_gather x2, waiting for transfers between devices, half_step(): whole = lax.all_gather(stacked, 'dev', axis=0, tiled=True)  324 us
    gather x32, local copies, waits for them, and re-layouts, collect(): picked = jnp.take(whole, row_index, axis=0).astype(jnp.float32)  128 us
    all_gather x4, blocking collectives, gather_in_order(): blocks = lax.all_gather(blocks, axes[k])  59.2 us
    concatenate x2, local copies, waits for them, and re-layouts, half_step(): rows = jnp.concatenate(row_parts, axis=1)  42.9 us
    dot_general x2, matrix products, gram_of(): lax.dot_general(block, block, (((0,), (0,)), ((), ())), preferred_element...  22.7 us
    dot_general x6, matrix products, apply(): jnp.einsum('usr,ur->us', rows, vector, precision=lax.Precision.HIGHEST)  18.5 us
    unnamed x9, other arithmetic  18 us
    unnamed x74, local copies, waits for them, and re-layouts  17.6 us
  transfers between devices with their start and end apart: 2, of which 2 were waited for; matrix products, arithmetic and copies ran while one was open for 2% of the time, Pallas kernels for 0%

commit v1 on v0

--- a/solution.py
+++ b/solution.py
@@ -76,7 +76,8 @@
     conf_parts = []
     mask_parts = []
     stacked = whole_of(packed, GRP, (0, 1), 0)
-    whole = lax.all_gather(stacked, "dev", axis=0, tiled=True)
+    outgoing = jnp.stack([stacked] * lax.axis_size("dev"))
+    whole = jnp.concatenate(lax.all_to_all(outgoing, "dev", 0, 0), axis=0)
     for span in range(groups):
         local = slot_ids[:, span, :]
         row_index = (

time: 751 us -> 827 us (1.10)
  the two profiles are of different devices: /device:TPU:1 before, /device:TPU:52 now
where the time goes in v1:
time: 827 us; the launch traced here: 814 us
  waiting for transfers between devices  405 us (49%)
  local copies, waits for them, and re-layouts  231 us (28%)
  matrix products  62.7 us (8%)
  other arithmetic  58.1 us (7%)
  blocking collectives  37.6 us (5%)
  starting transfers between devices  17.4 us (2%)
    all_to_all x2, waiting for transfers between devices, half_step(): whole = jnp.concatenate(lax.all_to_all(outgoing, 'dev', 0, 0), axis=0)  405 us
    gather x32, local copies, waits for them, and re-layouts, collect(): picked = jnp.take(whole, row_index, axis=0).astype(jnp.float32)  128 us
    concatenate x2, local copies, waits for them, and re-layouts, half_step(): rows = jnp.concatenate(row_parts, axis=1)  42.9 us
    all_gather x4, blocking collectives, gather_in_order(): blocks = lax.all_gather(blocks, axes[k])  37.6 us
    dot_general x2, matrix products, gram_of(): lax.dot_general(block, block, (((0,), (0,)), ((), ())), preferred_element...  22.5 us
    dot_general x6, matrix products, apply(): jnp.einsum('usr,ur->us', rows, vector, precision=lax.Precision.HIGHEST)  18.5 us
    unnamed x9, other arithmetic  18 us
    unnamed x78, local copies, waits for them, and re-layouts  17.6 us
  transfers between devices with their start and end apart: 2, of which 2 were waited for; matrix products, arithmetic and copies ran while one was open for 1% of the time, Pallas kernels for 0%

profile of v1, /device:TPU:52, one launch (start us, length us, event | category | flops | bytes accessed | tf_op | source)
XLA Modules:
  0.0 813.7 jit_solution(12083694416337913886)
XLA Ops:
  1.5 16.5 %all-gather = bf16[256,256]{1,0:T(8,128)(2,1)S(1)} all-gather(bf16[64,256]{1,0:T(8,128)(2,1)S(1)} %convert_element_type.189), channel_id=2, replica_groups=mesh['grp_0'=4,'grp_1'=2,'dev'=32] {'grp_0'}, dimensions={0}, use_global_device_ids=true | all-gather | bytes 163840 | tf_op jit(solution)/shard_map/all_gather | solution.py:22
  20.0 4.2 stack.6
  24.2 8.5 %all-to-all-start = ((bf16[32,512,256]{2,1,0:T(8,128)(2,1)}), bf16[32,512,256]{2,1,0:T(8,128)(2,1)}, u32[]{:S(2)}, u32[]{:S(2)}) async-start(bf16[32,512,256]{2,1,0:T(8,128)(2,1)} %stack.6), calls=%async_computation | async-start | bytes 16777216 | tf_op jit(solution)/shard_map/all_to_all | solution.py:80
  38.8 125.1 %all-to-all-done = bf16[32,512,256]{2,1,0:T(8,128)(2,1)} async-done(((bf16[32,512,256]{2,1,0:T(8,128)(2,1)}), bf16[32,512,256]{2,1,0:T(8,128)(2,1)}, u32[]{:S(2)}, u32[]{:S(2)}) %all-to-all-start) | async-done | bytes 8388640 | tf_op jit(solution)/shard_map/all_to_all | solution.py:80
  164.0 6.1 gather_fusion
  170.2 6.1 gather_fusion.1
  176.5 6.1 gather_fusion.2
  182.7 6.1 gather_fusion.3
  188.9 6.5 gather_fusion.4
  195.5 6.1 gather_fusion.5
  201.8 6.1 gather_fusion.6
  208.0 6.1 gather_fusion.7
  223.4 22.3 %concatenate.20 = f32[128,24,256]{2,1,0:T(8,128)S(1)} concatenate(f32[128,3,256]{2,1,0:T(4,128)} %convert_multiply_fusion.15, f32[128,3,256]{2,1,0:T(4,128)} %convert_multiply_fusion.14, f32[128,3,256]{2,1,0:T(4,128)} %convert_multiply_fusion.13, f32[128,3,256]{2,1,0:T(4,128)} %convert_multiply_fusion.12, f32[128,3,256]{2,1,0:T(4,128)} %convert_multiply_fusion.11, ...), dimensions={1} | concatenate | bytes 6291456 | tf_op jit(solution)/shard_map/concatenate | solution.py:90
  245.7 2.8 fusion.18
  251.6 8.2 %convolution_bitcast_fusion.1 = f32[256,256]{1,0:T(8,128)S(1)} fusion(bf16[32,512,256]{2,1,0:T(8,128)(2,1)} %all-to-all-done), kind=kOutput, calls=%fused_computation.27 | convolution fusion | flops 2147483648 | bytes 8650752 | tf_op jit(solution)/shard_map/dot_general | solution.py:61
  324.2 16.9 %all-gather.2 = bf16[512,256]{0,1:T(8,128)(2,1)S(1)} all-gather(bf16[128,256]{0,1:T(8,128)(2,1)S(1)} %get-tuple-element.36), channel_id=4, replica_groups=mesh['grp_0'=4,'grp_1'=2,'dev'=32] {'grp_0'}, dimensions={0}, use_global_device_ids=true | all-gather | bytes 327680 | tf_op jit(solution)/shard_map/all_gather | solution.py:22
  343.5 5.9 stack.7
  349.4 8.9 %all-to-all-start.1 = ((bf16[32,1024,256]{2,1,0:T(8,128)(2,1)}), bf16[32,1024,256]{2,1,0:T(8,128)(2,1)}, u32[]{:S(2)}, u32[]{:S(2)}) async-start(bf16[32,1024,256]{2,1,0:T(8,128)(2,1)} %stack.7), calls=%async_computation.1 | async-start | bytes 33554432 | tf_op jit(solution)/shard_map/all_to_all | solution.py:80
  363.9 279.8 %all-to-all-done.1 = bf16[32,1024,256]{2,1,0:T(8,128)(2,1)} async-done(((bf16[32,1024,256]{2,1,0:T(8,128)(2,1)}), bf16[32,1024,256]{2,1,0:T(8,128)(2,1)}, u32[]{:S(2)}, u32[]{:S(2)}) %all-to-all-start.1) | async-done | bytes 16777248 | tf_op jit(solution)/shard_map/all_to_all | solution.py:80
  643.7 9.6 %gather_fusion.8 = bf16[384,256]{1,0:T(8,128)(2,1)S(1)} fusion(bf16[32768,256]{1,0:T(8,128)(2,1)} %bitcast.57, s32[1024]{0:T(1024)S(1)} %pad_clamp_fusion.7), kind=kCustom, calls=%fused_computation.1.clone | custom fusion | bytes 394752 | tf_op jit(solution)/shard_map/jit(_take)/gather | solution.py:67
  653.3 9.6 %gather_fusion.9 = bf16[384,256]{1,0:T(8,128)(2,1)S(1)} fusion(bf16[32768,256]{1,0:T(8,128)(2,1)} %bitcast.57, s32[1024]{0:T(1024)S(1)} %pad_clamp_fusion.6), kind=kCustom, calls=%fused_computation.9.clone | custom fusion | bytes 394752 | tf_op jit(solution)/shard_map/jit(_take)/gather | solution.py:67
  663.0 10.0 %gather_fusion.10 = bf16[384,256]{1,0:T(8,128)(2,1)S(1)} fusion(bf16[32768,256]{1,0:T(8,128)(2,1)} %bitcast.57, s32[1024]{0:T(1024)S(1)} %pad_clamp_fusion.5), kind=kCustom, calls=%fused_computation.10.clone | custom fusion | bytes 394752 | tf_op jit(solution)/shard_map/jit(_take)/gather | solution.py:67
  673.1 9.6 %gather_fusion.11 = bf16[384,256]{1,0:T(8,128)(2,1)S(1)} fusion(bf16[32768,256]{1,0:T(8,128)(2,1)} %bitcast.57, s32[1024]{0:T(1024)S(1)} %pad_clamp_fusion.4), kind=kCustom, calls=%fused_computation.11.clone | custom fusion | bytes 394752 | tf_op jit(solution)/shard_map/jit(_take)/gather | solution.py:67
  682.8 9.6 %gather_fusion.12 = bf16[384,256]{1,0:T(8,128)(2,1)S(1)} fusion(bf16[32768,256]{1,0:T(8,128)(2,1)} %bitcast.57, s32[1024]{0:T(1024)S(1)} %pad_clamp_fusion.3), kind=kCustom, calls=%fused_computation.12.clone | custom fusion | bytes 394752 | tf_op jit(solution)/shard_map/jit(_take)/gather | solution.py:67
  692.5 9.6 %gather_fusion.13 = bf16[384,256]{1,0:T(8,128)(2,1)S(1)} fusion(bf16[32768,256]{1,0:T(8,128)(2,1)} %bitcast.57, s32[1024]{0:T(1024)S(1)} %pad_clamp_fusion.2), kind=kCustom, calls=%fused_computation.13.clone | custom fusion | bytes 394752 | tf_op jit(solution)/shard_map/jit(_take)/gather | solution.py:67
  702.2 9.8 %gather_fusion.14 = bf16[384,256]{1,0:T(8,128)(2,1)S(1)} fusion(bf16[32768,256]{1,0:T(8,128)(2,1)} %bitcast.57, s32[1024]{0:T(1024)S(1)} %pad_clamp_fusion.1), kind=kCustom, calls=%fused_computation.14.clone | custom fusion | bytes 394752 | tf_op jit(solution)/shard_map/jit(_take)/gather | solution.py:67
  712.0 9.6 %gather_fusion.15 = bf16[384,256]{1,0:T(8,128)(2,1)S(1)} fusion(bf16[32768,256]{1,0:T(8,128)(2,1)} %bitcast.57, s32[1024]{0:T(1024)S(1)} %pad_clamp_fusion), kind=kCustom, calls=%fused_computation.15.clone | custom fusion | bytes 394752 | tf_op jit(solution)/shard_map/jit(_take)/gather | solution.py:67
  729.7 20.6 %concatenate.23 = f32[64,48,256]{2,1,0:T(8,128)S(1)} concatenate(f32[64,6,256]{2,1,0:T(8,128)} %convert_multiply_fusion.7, f32[64,6,256]{2,1,0:T(8,128)} %convert_multiply_fusion.6, f32[64,6,256]{2,1,0:T(8,128)} %convert_multiply_fusion.5, f32[64,6,256]{2,1,0:T(8,128)} %convert_multiply_fusion.4, f32[64,6,256]{2,1,0:T(8,128)} %convert_multiply_fusion.3, ...), dimensions={1} | concatenate | bytes 6291456 | tf_op jit(solution)/shard_map/concatenate | solution.py:90
  757.8 14.3 %convolution_bitcast_fusion = f32[256,256]{1,0:T(8,128)S(1)} fusion(bf16[32,1024,256]{2,1,0:T(8,128)(2,1)} %all-to-all-done.1), kind=kOutput, calls=%fused_computation.26 | convolution fusion | flops 4294967296 | bytes 17039360 | tf_op jit(solution)/shard_map/dot_general | solution.py:61
  778.1 3.4 fusion.24
  790.0 3.4 fusion.22
  802.1 3.4 fusion.20
  (317 shorter events, 140.6 us)
Async XLA Ops:
  24.1 8.5 %copy-start.23 = (s32[128,8,3]{0,1,2:T(8,128)S(1)}, s32[128,8,3]{0,1,2:T(8,128)}, u32[]{:S(2)}) copy-start(s32[128,8,3]{0,1,2:T(8,128)} %param.14) | copy-start | bytes 36868
  24.1 8.9 %copy-start.24 = (s32[128,8,3]{0,1,2:T(8,128)S(1)}, s32[128,8,3]{0,1,2:T(8,128)}, u32[]{:S(2)}) copy-start(s32[128,8,3]{0,1,2:T(8,128)} %param.16) | copy-start | bytes 36868
  24.1 13.3 %copy-start.5 = (f32[128,256]{1,0:T(8,128)S(1)}, f32[128,256]{1,0:T(8,128)}, u32[]{:S(2)}) copy-start(f32[128,256]{1,0:T(8,128)} %param.12) | copy-start | bytes 393220
  24.1 14.1 %copy-start.25 = (f32[128,8,3]{0,1,2:T(8,128)S(1)}, f32[128,8,3]{0,1,2:T(8,128)}, u32[]{:S(2)}) copy-start(f32[128,8,3]{0,1,2:T(8,128)} %param.15) | copy-start | bytes 36868
  24.2 139.8 %all-to-all-start = ((bf16[32,512,256]{2,1,0:T(8,128)(2,1)}), bf16[32,512,256]{2,1,0:T(8,128)(2,1)}, u32[]{:S(2)}, u32[]{:S(2)}) async-start(bf16[32,512,256]{2,1,0:T(8,128)(2,1)} %stack.6), calls=%async_computation | async-start | bytes 16777216 | tf_op jit(solution)/shard_map/all_to_all | solution.py:80
  251.6 8.2 %copy-start.6 = (f32[128,256]{1,0:T(8,128)S(1)}, f32[128,256]{1,0:T(8,128)}, u32[]{:S(2)}) copy-start(f32[128,256]{1,0:T(8,128)} %param.12) | copy-start | bytes 393220
  251.6 8.2 %copy-start.7 = (f32[128,256]{0,1:T(8,128)S(1)}, f32[128,256]{0,1:T(8,128)}, u32[]{:S(2)}) copy-start(f32[128,256]{0,1:T(8,128)} %copy.252) | copy-start | bytes 393220
  251.6 8.2 %copy-start.17 = (f32[128,256]{0,1:T(8,128)S(1)}, f32[128,256]{0,1:T(8,128)}, u32[]{:S(2)}) copy-start(f32[128,256]{0,1:T(8,128)} %copy.311) | copy-start | bytes 393220
  251.6 8.2 %copy-start.18 = (f32[128,256]{0,1:T(8,128)S(1)}, f32[128,256]{0,1:T(8,128)}, u32[]{:S(2)}) copy-start(f32[128,256]{0,1:T(8,128)} %copy.318) | copy-start | bytes 393220
  272.8 0.7 copy-start
  272.8 0.6 copy-start.28
  288.2 1.0 copy-start.27
  289.2 1.2 copy-start.1
  306.0 2.1 copy-start.26
  349.4 8.9 %copy-start.20 = (s32[64,8,6]{0,1,2:T(8,128)S(1)}, s32[64,8,6]{0,1,2:T(8,128)}, u32[]{:S(2)}) copy-start(s32[64,8,6]{0,1,2:T(8,128)} %param.17) | copy-start | bytes 36868
  349.4 9.2 %copy-start.21 = (s32[64,8,6]{0,1,2:T(8,128)S(1)}, s32[64,8,6]{0,1,2:T(8,128)}, u32[]{:S(2)}) copy-start(s32[64,8,6]{0,1,2:T(8,128)} %param.19) | copy-start | bytes 36868
  349.4 12.7 %copy-start.22 = (f32[64,8,6]{0,1,2:T(8,128)S(1)}, f32[64,8,6]{0,1,2:T(8,128)}, u32[]{:S(2)}) copy-start(f32[64,8,6]{0,1,2:T(8,128)} %param.18) | copy-start | bytes 36868
  349.4 294.2 %all-to-all-start.1 = ((bf16[32,1024,256]{2,1,0:T(8,128)(2,1)}), bf16[32,1024,256]{2,1,0:T(8,128)(2,1)}, u32[]{:S(2)}, u32[]{:S(2)}) async-start(bf16[32,1024,256]{2,1,0:T(8,128)(2,1)} %stack.7), calls=%async_computation.1 | async-start | bytes 33554432 | tf_op jit(solution)/shard_map/all_to_all | solution.py:80
  729.7 20.6 %copy-start.14 = (f32[64,256]{1,0:T(8,128)S(1)}, f32[64,256]{1,0:T(8,128)}, u32[]{:S(2)}) copy-start(f32[64,256]{1,0:T(8,128)} %param.13) | copy-start | bytes 196612
  757.8 14.3 %copy-start.19 = (f32[64,1,256]{2,1,0:T(1,128)S(1)}, f32[64,1,256]{2,1,0:T(1,128)}, u32[]{:S(2)}) copy-start(f32[64,1,256]{2,1,0:T(1,128)} %fusion.191) | copy-start | bytes 196612
  772.4 2.8 copy-start.16
  777.4 0.6 copy-start.8
  785.7 2.8 copy-start.9
  788.7 0.6 copy-start.10
  789.4 0.6 copy-start.2
  797.6 2.7 copy-start.3
  797.6 3.0 copy-start.11
  801.4 0.6 copy-start.12
  802.1 10.4 %copy-start.32 = (f32[64]{0:T(128)S(1)}, f32[64]{0:T(128)}, u32[]{:S(2)}) copy-start(f32[64]{0:T(128)} %copy-done.31) | copy-start | bytes 772
  809.7 2.4 copy-start.13
  809.7 2.8 copy-start.4
  809.7 2.8 copy-start.15
  (3 other events, 1.6 us)
